TPU v7x, 32 devices: a whole 2x2x4 slice. The times are simulated.
32 devices in a mesh: member: 8 (over z, x), domain: 4 (over y, core).
Axes of the slice: x: 2, y: 2, z: 4, core: 2. Of those that a mesh axis runs over, the one named last changes fastest.
Arguments:
- starting_tracer_fields: float32 [8, 2, 8, 64, 640], P('member', None, None, 'domain'), may hold values from -6 to 6
- surface_exchange_inputs: float32 [8, 2, 64, 640], P('member', None, 'domain'), may hold values from -4 to 4
- diffusivity: float32 [2, 8], replicated, may hold values from 0.04 to 0.2
- mixing: float32 [2, 7], replicated, may hold values from 0.02 to 0.1
- land_mask: int32 [64, 640], replicated, may hold values 0 or 1
- obs_index: int32 [4, 8, 256], P('domain'), may hold values from 0 to 1279
- obs_count: int32 [4, 8], P('domain'), may hold values from 1 to 256, as said below
- obs_value: float32 [4, 8, 256], P('domain'), may hold values from -8 to 8
- obs_error: float32 [4, 8, 256], P('domain'), may hold values from 1 to 16
Outputs:
- analysis: float32 [8, 2, 8, 64, 640], P('member', None, None, 'domain')
Inputs may be any that keep to these rules, and one draw needn't show every extreme that they name: `obs_index`: A cell of the tile's 2 x 640 surface cells, counted row by row. `obs_count`: slots below the count hold observations, the rest are unused; in every domain the last tile holds exactly 256.
All inputs are finite; a program needn't handle non-finite values.
Results may differ from a plain program's by a relative error of at most 0.0001.
Values sent between devices are 32-bit elements; how exact they have to be, the bound alone decides.
A program may use at most 64 MiB of HBM per device.

v0:
```python
import jax
import jax.numpy as jnp
from jax import lax
from jax.sharding import PartitionSpec as P

STEPS = 2


def with_halo(shard, sides, width):
    for axis, dim in sides:
        size, length = (lax.axis_size(axis), shard.shape[dim])
        up = [(i, (i + 1) % size) for i in range(size - 1)]
        down = [(j, i) for i, j in up]
        last = lax.slice_in_dim(shard, length - width, length, axis=dim)
        initial = lax.slice_in_dim(shard, 0, width, axis=dim)
        before = lax.ppermute(last, axis, up)
        after = lax.ppermute(initial, axis, down)
        shard = jnp.concatenate([before, shard, after], axis=dim)
    return shard


def stencil(padded, mask_rows, diffusivity, mixing, surface_exchange_inputs):
    middle = padded[:, :, 1:-1]
    mask_mid = mask_rows[1:-1]
    upper_row = padded[:, :, 2:]
    lower_row = padded[:, :, :-2]
    east_cell = jnp.roll(middle, -1, axis=3)
    west_cell = jnp.roll(middle, 1, axis=3)
    lateral = mask_rows[2:] * (upper_row - middle) + mask_rows[:-2] * (lower_row - middle)
    lateral = lateral + jnp.roll(mask_mid, -1, axis=1) * (east_cell - middle)
    lateral = lateral + jnp.roll(mask_mid, 1, axis=1) * (west_cell - middle)
    downward_flux = mixing[:, :, None, None] * (middle[:, 1:] - middle[:, :-1])
    empty_level = jnp.zeros_like(middle[:, :1])
    vertical = jnp.concatenate([downward_flux, empty_level], axis=1) - jnp.concatenate(
        [empty_level, downward_flux], axis=1
    )
    tendency = diffusivity[:, :, None, None] * lateral + vertical
    tendency = tendency.at[:, 0].add(surface_exchange_inputs)
    return middle + mask_mid * tendency


def partial_sums(observed, values, errors, active):
    average = jnp.mean(observed, axis=0)
    anomaly = observed - average[None, :]
    weight_obs = active / errors
    gram = jnp.dot(anomaly * weight_obs[None, :], anomaly.T, precision=lax.Precision.HIGHEST)
    pull = jnp.dot(anomaly, weight_obs * (values - average), precision=lax.Precision.HIGHEST)
    return (gram, pull)


def transform(gram, pull):
    count = gram.shape[0]
    identity = jnp.eye(count, dtype=gram.dtype)
    factor = jnp.linalg.cholesky(gram + (count - 1.0) * identity)
    inverse = jax.scipy.linalg.solve_triangular(factor, identity, lower=True)
    mean_weight = jnp.dot(
        inverse.T,
        jnp.dot(inverse, pull, precision=lax.Precision.HIGHEST),
        precision=lax.Precision.HIGHEST,
    )
    weights = mean_weight[:, None] + jnp.sqrt(count - 1.0) * inverse.T
    return weights - jnp.mean(weights, axis=0, keepdims=True) + 1.0 / count


def update(kernel, tile_block, tile_mask):
    count = tile_block.shape[0]
    updated = jnp.einsum(
        "jm,jn->mn", kernel, tile_block.reshape(count, -1), precision=lax.Precision.HIGHEST
    )
    return jnp.where(tile_mask > 0, updated.reshape(tile_block.shape), tile_block)


def shards(
    starting_tracer_fields,
    surface_exchange_inputs,
    diffusivity,
    mixing,
    land_mask,
    obs_index,
    obs_count,
    obs_value,
    obs_error,
):
    ocean_state = starting_tracer_fields[0]
    row_count = ocean_state.shape[2]
    longitudes = ocean_state.shape[3]
    subregion_offset = lax.axis_index("domain")
    sea_mask = land_mask.astype(jnp.float32)
    padded_mask = jnp.pad(sea_mask, ((1, 1), (0, 0)))
    local_mask = lax.dynamic_slice_in_dim(
        padded_mask, subregion_offset * row_count, row_count + 2, 0
    )
    for _ in range(STEPS):
        padded = with_halo(ocean_state, (("domain", 2),), 1)
        ocean_state = stencil(padded, local_mask, diffusivity, mixing, surface_exchange_inputs[0])
    stacked = ocean_state.reshape(1, -1, row_count, longitudes)
    members = lax.axis_size("member")
    tile_rows = row_count // members
    tile_index = lax.axis_index("member")
    tile_mask = lax.dynamic_slice_in_dim(local_mask[1:-1], tile_index * tile_rows, tile_rows, 0)
    slot_rank = jnp.arange(obs_index.shape[2], dtype=jnp.int32)
    tile_block = lax.all_to_all(stacked, "member", split_axis=2, concat_axis=0, tiled=True)
    surface = tile_block[:, 0].reshape(members, -1)
    obs_slots = lax.dynamic_index_in_dim(obs_index[0], tile_index, 0, keepdims=False)
    observed = surface[:, obs_slots]
    limit = lax.dynamic_index_in_dim(obs_count[0], tile_index, 0, keepdims=False)
    active = (slot_rank < limit).astype(jnp.float32)
    values = lax.dynamic_index_in_dim(obs_value[0], tile_index, 0, keepdims=False)
    errors = lax.dynamic_index_in_dim(obs_error[0], tile_index, 0, keepdims=False)
    gram, pull = partial_sums(observed, values, errors, active)
    gram, pull = lax.psum((gram, pull), "member")
    kernel = transform(gram, pull)
    updated = update(kernel, tile_block, tile_mask)
    returned = lax.all_to_all(updated, "member", split_axis=0, concat_axis=2, tiled=True)
    return returned.reshape(starting_tracer_fields.shape)


def solution(mesh):
    placed = (
        P("member", None, None, "domain", None),
        P("member", None, "domain", None),
        P(),
        P(),
        P(),
        P("domain", None, None),
        P("domain", None),
        P("domain", None, None),
        P("domain", None, None),
    )
    return jax.shard_map(
        shards,
        mesh=mesh,
        in_specs=placed,
        out_specs=P("member", None, None, "domain", None),
        check_vma=False,
    )
```

profile of v0, /device:TPU:0, one launch (start us, length us, event | category | flops | bytes accessed | tf_op | source)
XLA Modules:
  0.0 90.1 jit_solution(5743181250172521186)
XLA Ops:
  0.0 0.0 copy-start
  0.0 0.0 copy-start.1
  0.0 1.2 %fusion.61 = (f32[2,8,1,640]{3,2,1,0:T(1,128)S(1)}, f32[2,8,1,640]{3,2,1,0:T(1,128)S(1)}) fusion(f32[2,8,16,640]{3,2,1,0:T(8,128)} %bitcast.78), kind=kLoop, calls=%fused_computation.108 | loop fusion | bytes 163840 | tf_op jit(solution)/shard_map/slice | solution.py:15
  1.2 1.3 %collective-permute-start = (f32[2,8,1,640]{3,2,1,0:T(1,128)S(1)}, f32[2,8,1,640]{3,2,1,0:T(1,128)S(1)}, u32[]{:S(2)}, u32[]{:S(2)}) collective-permute-start(f32[2,8,1,640]{3,2,1,0:T(1,128)S(1)} %get-tuple-element.43), channel_id=1, source_target_pairs={{1,0},{2,1},{3,2},{5,4},{6,5},{7,6},{9,8},{10,9},{11,10},{13,12},{... | collective-permute-start | bytes 122888 | tf_op jit(solution)/shard_map/ppermute | solution.py:17
  2.5 3.0 %collective-permute-start.1 = (f32[2,8,1,640]{3,2,1,0:T(1,128)S(1)}, f32[2,8,1,640]{3,2,1,0:T(1,128)S(1)}, u32[]{:S(2)}, u32[]{:S(2)}) collective-permute-start(f32[2,8,1,640]{3,2,1,0:T(1,128)S(1)} %get-tuple-element.44), channel_id=1, source_target_pairs={{0,1},{1,2},{2,3},{4,5},{5,6},{6,7},{8,9},{9,10},{10,11},{12,13},{... | collective-permute-start | bytes 122888 | tf_op jit(solution)/shard_map/ppermute | solution.py:16
  5.5 1.1 %fusion.59 = (f32[2,8,16,1]{3,2,1,0:T(8,128)S(1)}, f32[2,8,16,1]{3,2,1,0:T(8,128)S(1)}) fusion(f32[2,8,16,640]{3,2,1,0:T(8,128)} %bitcast.79), kind=kLoop, calls=%fused_computation.106 | loop fusion | bytes 4096 | tf_op jit(solution)/shard_map/jit(_roll_static)/slice | solution.py:28
  6.6 0.0 copy-done.1
  6.6 0.0 copy-start.3
  6.6 0.2 fusion.60
  6.9 0.7 copy-done.3
  7.6 0.1 pad_dynamic-slice_fusion.1
  7.7 0.1 pad_dynamic-slice_fusion.2
  7.7 0.0 copy-start.4
  7.8 0.6 copy-done.4
  8.4 0.1 fusion.25
  8.5 0.1 pad_maximum_fusion.4
  8.6 0.0 collective-permute-done
  8.6 0.0 collective-permute-done.1
  8.6 0.0 copy-start.5
  8.7 0.7 copy-done.5
  9.3 0.6 fusion.15
  9.9 0.3 copy-done.2
  10.2 0.1 multiply_add_fusion.1
  10.3 0.1 fusion.58
  10.4 0.1 fusion.24
  10.5 0.2 fusion.57
  10.8 1.3 %collective-permute-start.2 = (f32[2,8,1,640]{3,2,1,0:T(1,128)S(1)}, f32[2,8,1,640]{3,2,1,0:T(1,128)S(1)}, u32[]{:S(2)}, u32[]{:S(2)}) collective-permute-start(f32[2,8,1,640]{3,2,1,0:T(1,128)S(1)} %get-tuple-element.37), channel_id=1, source_target_pairs={{1,0},{2,1},{3,2},{5,4},{6,5},{7,6},{9,8},{10,9},{11,10},{13,12},{... | collective-permute-start | bytes 122888 | tf_op jit(solution)/shard_map/ppermute | solution.py:17
  12.1 5.1 %collective-permute-start.3 = (f32[2,8,1,640]{3,2,1,0:T(1,128)S(1)}, f32[2,8,1,640]{3,2,1,0:T(1,128)S(1)}, u32[]{:S(2)}, u32[]{:S(2)}) collective-permute-start(f32[2,8,1,640]{3,2,1,0:T(1,128)S(1)} %get-tuple-element.38), channel_id=1, source_target_pairs={{0,1},{1,2},{2,3},{4,5},{5,6},{6,7},{8,9},{9,10},{10,11},{12,13},{... | collective-permute-start | bytes 122888 | tf_op jit(solution)/shard_map/ppermute | solution.py:16
  17.2 0.1 fusion.56
  17.3 0.0 collective-permute-done.2
  17.3 0.7 collective-permute-done.3
  18.1 0.6 fusion.6
  18.7 0.1 multiply_add_fusion
  18.8 1.0 %copy.32 = f32[1,16,16,640]{3,1,0,2:T(8,128)} copy(f32[1,16,16,640]{3,2,1,0:T(8,128)S(1)} %bitcast.85) | data formatting | bytes 1310720 | tf_op jit(solution)/shard_map/reshape | solution.py:96
  19.8 5.8 %all-to-all-start = ((f32[1,16,16,640]{3,1,0,2:T(8,128)}), f32[1,16,16,640]{3,1,0,2:T(8,128)S(1)}, u32[]{:S(2)}, u32[]{:S(2)}) async-start(f32[1,16,16,640]{3,1,0,2:T(8,128)} %copy.32), calls=%async_computation | async-start | bytes 1310720 | tf_op jit(solution)/shard_map/all_to_all | solution.py:102
  25.6 0.0 copy-done
  25.6 0.6 constant_dynamic-slice_fusion.2
  26.2 0.7 compare_select_fusion
  26.9 0.7 constant_dynamic-slice_fusion
  27.7 15.9 %all-to-all-done = f32[1,16,16,640]{3,1,0,2:T(8,128)S(1)} async-done(((f32[1,16,16,640]{3,1,0,2:T(8,128)}), f32[1,16,16,640]{3,1,0,2:T(8,128)S(1)}, u32[]{:S(2)}, u32[]{:S(2)}) %all-to-all-start) | async-done | bytes 655392 | tf_op jit(solution)/shard_map/all_to_all | solution.py:102
  43.6 0.4 copy.55
  44.0 0.2 copy.34
  44.2 0.7 gather_fusion
  45.0 0.1 reduce_sum.18
  45.1 0.6 subtract_multiply_fusion
  45.7 0.2 convolution_bitcast_fusion.2
  46.0 0.5 fusion.27
  46.5 20.4 %all-reduce.5 = (f32[8,8]{0,1:T(8,128)S(1)}, f32[8]{0:T(128)S(1)}) all-reduce(f32[8,8]{0,1:T(8,128)S(1)} %fusion.27, f32[8]{0:T(128)S(1)} %convolution_bitcast_fusion.2), channel_id=1, replica_groups=mesh['member'=8,'domain'=4] {'member'}, use_global_device_ids=true, to_apply=%region_1.2 | all-reduce | flops 72 | bytes 576 | tf_op jit(solution)/shard_map/psum | solution.py:111
  66.9 0.1 copy.36
  67.0 0.7 cholesky.17
  67.7 0.1 copy.37
  67.8 0.1 select_reduce_fusion
  67.9 0.6 compare_reduce_fusion
  68.6 0.6 select_select_fusion
  69.2 0.1 copy.39
  69.3 0.6 custom-call.7
  69.9 0.1 fusion.36
  70.0 0.1 convolution_bitcast_fusion.1
  70.2 0.1 convolution_bitcast_fusion
  70.3 0.1 fusion.45
  70.4 1.4 %convolution_select_fusion = f32[8,16,2,640]{3,0,2,1:T(8,128)S(1)} fusion(f32[1,16,8,2,640]{4,1,3,2,0:T(8,128)S(1)} %bitcast.84, pred[2,640]{1,0:T(4,128)(4,1)S(1)} %fusion.35, f32[8,8]{0,1:T(8,128)S(1)} %fusion.36, f32[8]{0:T(128)S(1)} %broadcast_multiply_fusion.1, f32[8]{0:T(128)S(1)} %convolution_bitcast_fusion), kind=kOutput, calls=%fused_computation.1 | convolution fusion | flops 15892736 | bytes 1312320 | tf_op jit(solution)/shard_map/jm,jn->mn/dot_general | solution.py:67
  71.8 0.3 copy.42
  72.2 16.9 %all_to_all.33 = f32[8,16,2,640]{3,2,1,0:T(2,128)S(1)} all-to-all(f32[8,16,2,640]{3,2,1,0:T(2,128)S(1)} %copy.42), channel_id=1, replica_groups=mesh['member'=8,'domain'=4] {'member'}, dimensions={0} | all-to-all | bytes 1310720 | tf_op jit(solution)/shard_map/all_to_all | solution.py:114
  89.1 1.0 %copy.44 = f32[1,2,8,16,640]{4,3,2,1,0:T(8,128)} copy(f32[1,2,8,16,640]{4,2,1,3,0:T(8,128)S(1)} %bitcast.86) | data formatting | bytes 1310720 | tf_op jit(solution)/shard_map/reshape | solution.py:115
  (12 shorter events, 0.2 us)
Async XLA Ops:
  0.0 25.6 %copy-start = (s32[1,8]{1,0:T(1,128)S(1)}, s32[1,8]{1,0:T(1,128)}, u32[]{:S(2)}) copy-start(s32[1,8]{1,0:T(1,128)} %param.19) | copy-start | bytes 100
  0.0 6.6 %copy-start.1 = (f32[1,2,8,16,640]{4,3,2,1,0:T(8,128)S(1)}, f32[1,2,8,16,640]{4,3,2,1,0:T(8,128)}, u32[]{:S(2)}) copy-start(f32[1,2,8,16,640]{4,3,2,1,0:T(8,128)} %param.13) | copy-start | bytes 1966084
  1.2 7.4 %collective-permute-start = (f32[2,8,1,640]{3,2,1,0:T(1,128)S(1)}, f32[2,8,1,640]{3,2,1,0:T(1,128)S(1)}, u32[]{:S(2)}, u32[]{:S(2)}) collective-permute-start(f32[2,8,1,640]{3,2,1,0:T(1,128)S(1)} %get-tuple-element.43), channel_id=1, source_target_pairs={{1,0},{2,1},{3,2},{5,4},{6,5},{7,6},{9,8},{10,9},{11,10},{13,12},{... | collective-permute-start | bytes 122888 | tf_op jit(solution)/shard_map/ppermute | solution.py:17
  2.5 6.1 %collective-permute-start.1 = (f32[2,8,1,640]{3,2,1,0:T(1,128)S(1)}, f32[2,8,1,640]{3,2,1,0:T(1,128)S(1)}, u32[]{:S(2)}, u32[]{:S(2)}) collective-permute-start(f32[2,8,1,640]{3,2,1,0:T(1,128)S(1)} %get-tuple-element.44), channel_id=1, source_target_pairs={{0,1},{1,2},{2,3},{4,5},{5,6},{6,7},{8,9},{9,10},{10,11},{12,13},{... | collective-permute-start | bytes 122888 | tf_op jit(solution)/shard_map/ppermute | solution.py:16
  6.6 0.9 %copy-start.3 = (s32[64,640]{1,0:T(8,128)S(1)}, s32[64,640]{1,0:T(8,128)}, u32[]{:S(2)}) copy-start(s32[64,640]{1,0:T(8,128)} %param.17) | copy-start | bytes 491524
  7.7 0.7 copy-start.4
  8.6 0.7 copy-start.5
  9.3 0.9 copy-start.2
  10.8 6.6 %collective-permute-start.2 = (f32[2,8,1,640]{3,2,1,0:T(1,128)S(1)}, f32[2,8,1,640]{3,2,1,0:T(1,128)S(1)}, u32[]{:S(2)}, u32[]{:S(2)}) collective-permute-start(f32[2,8,1,640]{3,2,1,0:T(1,128)S(1)} %get-tuple-element.37), channel_id=1, source_target_pairs={{1,0},{2,1},{3,2},{5,4},{6,5},{7,6},{9,8},{10,9},{11,10},{13,12},{... | collective-permute-start | bytes 122888 | tf_op jit(solution)/shard_map/ppermute | solution.py:17
  12.1 6.0 %collective-permute-start.3 = (f32[2,8,1,640]{3,2,1,0:T(1,128)S(1)}, f32[2,8,1,640]{3,2,1,0:T(1,128)S(1)}, u32[]{:S(2)}, u32[]{:S(2)}) collective-permute-start(f32[2,8,1,640]{3,2,1,0:T(1,128)S(1)} %get-tuple-element.38), channel_id=1, source_target_pairs={{0,1},{1,2},{2,3},{4,5},{5,6},{6,7},{8,9},{9,10},{10,11},{12,13},{... | collective-permute-start | bytes 122888 | tf_op jit(solution)/shard_map/ppermute | solution.py:16
  19.8 23.8 %all-to-all-start = ((f32[1,16,16,640]{3,1,0,2:T(8,128)}), f32[1,16,16,640]{3,1,0,2:T(8,128)S(1)}, u32[]{:S(2)}, u32[]{:S(2)}) async-start(f32[1,16,16,640]{3,1,0,2:T(8,128)} %copy.32), calls=%async_computation | async-start | bytes 1310720 | tf_op jit(solution)/shard_map/all_to_all | solution.py:102
where the time goes:
time: 90.7 us; the launch traced here: 90.1 us
  blocking collectives  37.3 us (41%)
  waiting for transfers between devices  16.7 us (18%)
  starting transfers between devices  16.6 us (18%)
  local copies, waits for them, and re-layouts  10.7 us (12%)
  other arithmetic  6.05 us (7%)
  matrix products  2.55 us (3%)
    psum x1, blocking collectives, shards(): gram, pull = lax.psum((gram, pull), 'member')  20.4 us
    all_to_all x1, blocking collectives, shards(): lax.all_to_all(updated, 'member', split_axis=0, concat_axis=2, tiled=True)  16.9 us
    all_to_all x1, waiting for transfers between devices, shards(): lax.all_to_all(stacked, 'member', split_axis=2, concat_axis=0, tiled=True)  15.9 us
    ppermute x2, starting transfers between devices, with_halo(): before = lax.ppermute(last, axis, up)  8.18 us
    all_to_all x1, starting transfers between devices, shards(): lax.all_to_all(stacked, 'member', split_axis=2, concat_axis=0, tiled=True)  5.81 us
    ppermute x2, starting transfers between devices, with_halo(): after = lax.ppermute(initial, axis, down)  2.58 us
    unnamed x12, local copies, waits for them, and re-layouts  2.27 us
  transfers between devices with their start and end apart: 5, of which 2 were waited for; matrix products, arithmetic and copies ran while one was open for 4% of the time, Pallas kernels for 0%

commit v1 on v0

v1 whole, which is shorter than its diff:
```python
import functools

import jax
import jax.numpy as jnp
from jax import lax
from jax.experimental import pallas as pl
from jax.experimental.pallas import tpu as pltpu
from jax.sharding import PartitionSpec as P

STEPS = 2
SUB = 8
LANES = 128
EXACT = lax.Precision.HIGHEST
MESH = pl.DeviceIdType.MESH
NT = (((1,), (1,)), ((), ()))


def masks(mask, table):
    rows, width = mask.shape
    table[0] = mask
    table[1] = pltpu.roll(mask, rows - 1, 0)
    table[2] = pltpu.roll(mask, 1, 0)
    table[3] = pltpu.roll(mask, width - 1, 1)
    table[4] = pltpu.roll(mask, 1, 1)


def step(source, target, table, flux, diffusivity, mixing):
    fields, levels = diffusivity.shape
    rows, width = source.shape[1:]

    def one(f, carry):
        above = None
        for l in range(levels):
            x = source[f * levels + l]
            lateral = table[1] * (pltpu.roll(x, rows - 1, 0) - x)
            lateral += table[2] * (pltpu.roll(x, 1, 0) - x)
            lateral += table[3] * (pltpu.roll(x, width - 1, 1) - x)
            lateral += table[4] * (pltpu.roll(x, 1, 1) - x)
            change = diffusivity[f, l] * lateral
            if l < levels - 1:
                down = mixing[f, l] * (source[f * levels + l + 1] - x)
                change += down
            if l > 0:
                change -= above
            else:
                change += flux[f]
            above = down
            target[f * levels + l] = x + table[0] * change
        return carry

    lax.fori_loop(0, fields, one, 0)


def body(
    members, domains, x_hbm, flux_hbm, mask_hbm, index_hbm, value_hbm, error_hbm,
    count, diffusivity, mixing, out,
    x, flux, land, index, value, error, mid, fore, table,
    halo_out, halo_in, edge, edge_mid, edge_flux, edge_table,
    sent, got, rhs, sums_out, sums_in, spread, tile_mask, reply,
    load_sem, halo_send, halo_recv, fore_send, fore_recv,
    sums_send, sums_recv, reply_send, reply_recv,
):
    me = lax.axis_index("member")
    domain = lax.axis_index("domain")
    parts, rows, width = x.shape
    fields = flux.shape[0]
    chunks = got.shape[0]
    tile_rows = rows // members
    per_chunk = SUB // tile_rows
    lat = mask_hbm.shape[0]
    first = domain == 0
    last = domain == domains - 1
    start_row = pl.multiple_of(domain * rows, SUB)
    above_row = pl.multiple_of(jnp.maximum(domain * rows - SUB, 0), SUB)
    below_row = pl.multiple_of(jnp.minimum(domain * rows + rows, lat - SUB), SUB)

    loads = [
        pltpu.make_async_copy(a, b, load_sem.at[i])
        for i, (a, b) in enumerate((
            (x_hbm, x),
            (flux_hbm, flux),
            (mask_hbm.at[pl.ds(above_row, SUB)], land.at[pl.ds(0, SUB)]),
            (mask_hbm.at[pl.ds(start_row, rows)], land.at[pl.ds(SUB, rows)]),
            (mask_hbm.at[pl.ds(below_row, SUB)], land.at[pl.ds(SUB + rows, SUB)]),
            (index_hbm, index),
            (value_hbm, value),
            (error_hbm, error),
        ))
    ]
    for load in loads:
        load.start()

    barrier = pltpu.get_barrier_semaphore()

    def greet(i, carry):
        peer = lax.rem(me + i, members)
        pl.semaphore_signal(barrier, inc=1, device_id={"member": peer}, device_id_type=MESH)
        return carry

    @pl.when(jnp.logical_not(first))
    def _():
        pl.semaphore_signal(barrier, inc=1, device_id={"domain": domain - 1}, device_id_type=MESH)

    @pl.when(jnp.logical_not(last))
    def _():
        pl.semaphore_signal(barrier, inc=1, device_id={"domain": domain + 1}, device_id_type=MESH)

    lax.fori_loop(1, members, greet, 0)
    for load in loads:
        load.wait()

    for p in range(parts):
        halo_out[0, 2 * p : 2 * p + 2] = x[p, 0:2]
        halo_out[1, 2 * p : 2 * p + 2] = x[p, rows - 2 : rows]
    for f in range(fields):
        at = 2 * (parts + f)
        halo_out[0, at : at + 2] = flux[f, 0:2]
        halo_out[1, at : at + 2] = flux[f, rows - 2 : rows]
    masks(land[SUB : SUB + rows].astype(jnp.float32), table)
    step(x, mid, table, flux, diffusivity, mixing)
    step(mid, fore, table, flux, diffusivity, mixing)

    def pack(tile):
        for p in range(parts):
            k = (p % per_chunk) * tile_rows
            sent[p // per_chunk, tile, k : k + tile_rows] = fore[
                p, tile * tile_rows : (tile + 1) * tile_rows
            ]

    for tile in range(1, members - 1):
        pack(tile)

    greeted = members - 1 + (1 - first.astype(jnp.int32)) + (1 - last.astype(jnp.int32))
    pl.semaphore_wait(barrier, greeted)

    to_upper = pltpu.make_async_remote_copy(
        halo_out.at[0], halo_in.at[1], halo_send.at[0], halo_recv.at[1],
        device_id={"domain": jnp.maximum(domain - 1, 0)}, device_id_type=MESH,
    )
    to_lower = pltpu.make_async_remote_copy(
        halo_out.at[1], halo_in.at[0], halo_send.at[1], halo_recv.at[0],
        device_id={"domain": jnp.minimum(domain + 1, domains - 1)}, device_id_type=MESH,
    )

    @pl.when(jnp.logical_not(first))
    def _():
        to_upper.start()

    @pl.when(jnp.logical_not(last))
    def _():
        to_lower.start()

    def send(chunk, peer):
        pltpu.make_async_remote_copy(
            sent.at[chunk, peer], got.at[chunk, me], fore_send, fore_recv.at[chunk],
            device_id={"member": peer}, device_id_type=MESH,
        ).start()

    early = (chunks + 1) // 2

    def send_all(low, high, wanted):
        def one(i, carry):
            chunk = low + i // (members - 1)
            peer = lax.rem(me + 1 + lax.rem(i, members - 1), members)

            @pl.when(wanted(peer))
            def _():
                send(chunk, peer)

            return carry

        lax.fori_loop(0, (high - low) * (members - 1), one, 0)

    send_all(0, early, lambda t: jnp.logical_and(t > 0, t < members - 1))

    @pl.when(first)
    def _():
        halo_in[0] = jnp.zeros_like(halo_in[0])

    @pl.when(last)
    def _():
        halo_in[1] = jnp.zeros_like(halo_in[1])

    half = SUB
    land_f = land[...].astype(jnp.float32)
    upper = land_f[SUB - 2 : SUB] * (1.0 - first.astype(jnp.float32))
    lower = land_f[SUB + rows : SUB + rows + 2] * (1.0 - last.astype(jnp.float32))
    masks(
        jnp.concatenate(
            [upper, land_f[SUB : SUB + 6], land_f[SUB + rows - 6 : SUB + rows], lower], axis=0
        ),
        edge_table,
    )
    for p in range(parts):
        edge[p, 2:half] = x[p, 0:6]
        edge[p, half : half + 6] = x[p, rows - 6 : rows]
    for f in range(fields):
        edge_flux[f, 2:half] = flux[f, 0:6]
        edge_flux[f, half : half + 6] = flux[f, rows - 6 : rows]

    @pl.when(jnp.logical_not(first))
    def _():
        to_lower.wait_recv()

    @pl.when(jnp.logical_not(last))
    def _():
        to_upper.wait_recv()

    for p in range(parts):
        edge[p, 0:2] = halo_in[0, 2 * p : 2 * p + 2]
        edge[p, half + 6 : half + 8] = halo_in[1, 2 * p : 2 * p + 2]
    for f in range(fields):
        at = 2 * (parts + f)
        edge_flux[f, 0:2] = halo_in[0, at : at + 2]
        edge_flux[f, half + 6 : half + 8] = halo_in[1, at : at + 2]
    step(edge, edge_mid, edge_table, edge_flux, diffusivity, mixing)
    step(edge_mid, edge, edge_table, edge_flux, diffusivity, mixing)
    for p in range(parts):
        fore[p, 0:2] = edge[p, 2:4]
        fore[p, rows - 2 : rows] = edge[p, half + 4 : half + 6]
    pack(0)
    pack(members - 1)
    send_all(0, early, lambda t: jnp.logical_or(t == 0, t == members - 1))
    for c in range(chunks):
        got[c, me] = sent[c, me]

    slots = index.shape[1]
    rank = lax.broadcasted_iota(jnp.int32, (1, slots), 1)
    active = (rank < count[0, me]).astype(jnp.float32)
    weight = active / error[pl.ds(me, 1), :]
    pair = jnp.concatenate(
        [weight, weight * value[pl.ds(me, 1), :], jnp.zeros((SUB - 2, slots), jnp.float32)], axis=0
    )
    where = index[pl.ds(me, 1), :]
    cells = []
    for r in range(tile_rows):
        cell = lax.broadcasted_iota(jnp.int32, (width, slots), 0) + r * width
        hit = (cell == where).astype(jnp.float32)
        cells.append(
            lax.dot_general(pair, hit, NT, precision=EXACT, preferred_element_type=jnp.float32)
        )
    rhs[...] = jnp.zeros_like(rhs)
    for k in range(SUB):
        at = SUB + me * tile_rows + k % tile_rows
        tile_mask[k : k + 1] = land[pl.ds(at, 1), :].astype(jnp.float32)

    def arrived(buffer, semaphore):
        pltpu.make_async_copy(buffer, buffer, semaphore).wait()

    arrived(got.at[0, pl.ds(0, members - 1)], fore_recv.at[0])

    sums = None
    for r in range(tile_rows):
        surface = jnp.concatenate([got[0, m, r : r + 1] for m in range(members)], axis=0)
        average = jnp.mean(surface, axis=0, keepdims=True)
        anomaly = surface - average
        cell_weight = cells[r][0:1]
        rhs[0:members] = anomaly * cell_weight
        rhs[members : members + 1] = cells[r][1:2] - cell_weight * average
        partial = lax.dot_general(
            anomaly, rhs[...], NT, precision=EXACT, preferred_element_type=jnp.float32
        )
        sums = partial if sums is None else sums + partial
    sums_out[...] = sums
    sums_in[me] = sums

    def send_sums(i, carry):
        peer = lax.rem(me + i, members)
        pltpu.make_async_remote_copy(
            sums_out, sums_in.at[me], sums_send, sums_recv,
            device_id={"member": peer}, device_id_type=MESH,
        ).start()
        return carry

    lax.fori_loop(1, members, send_sums, 0)
    send_all(early, chunks, lambda t: t >= 0)
    arrived(sums_in.at[pl.ds(0, members - 1)], sums_recv)

    total = sums_in[0]
    for m in range(1, members):
        total += sums_in[m]
    row = lax.broadcasted_iota(jnp.int32, total.shape, 0)
    lane = lax.broadcasted_iota(jnp.int32, total.shape, 1)
    system = total + jnp.where(lane == row, members - 1.0, 0.0)
    system = jnp.where(lane > members, jnp.where(lane == row + members + 1, 1.0, 0.0), system)

    def eliminate(k, a):
        pivot_row = jnp.sum(jnp.where(row == k, a, 0.0), axis=0, keepdims=True)
        column = jnp.sum(jnp.where(lane == k, a, 0.0), axis=1, keepdims=True)
        pivot = jnp.sum(jnp.where(lane[0:1] == k, pivot_row, 0.0), axis=1, keepdims=True)
        root = jnp.sqrt(pivot)
        return jnp.where(
            row == k, a / root, jnp.where(row > k, a - (column / pivot) * pivot_row, a)
        )

    system = lax.fori_loop(0, members, eliminate, system)
    inner = jnp.sum(jnp.where(lane == members, system, 0.0), axis=1, keepdims=True)
    mean_weight = jnp.sum(system * inner, axis=0, keepdims=True)
    weights = mean_weight + jnp.sqrt(jnp.float32(members - 1.0)) * system
    own = jnp.logical_and(lane > members, lane <= 2 * members)
    weights = jnp.where(own, weights, 0.0)
    weights = weights - jnp.sum(weights, axis=1, keepdims=True) / members + 1.0 / members
    for j in range(members):
        column = jnp.sum(jnp.where(lane == members + 1 + j, weights, 0.0), axis=1, keepdims=True)
        spread[j] = jnp.broadcast_to(column, (members, LANES))

    for c in range(chunks):
        if c > 0:
            arrived(got.at[c, pl.ds(0, members - 1)], fore_recv.at[c])

        def update(m, carry):
            for q in range(width // LANES):
                part = pl.ds(q * LANES, LANES)
                acc = None
                for j in range(members):
                    term = spread[j, pl.ds(m, 1), :] * got[c, j, :, part]
                    acc = term if acc is None else acc + term
                reply[c, m, :, part] = jnp.where(
                    tile_mask[:, part] > 0, acc, got[c, m, :, part]
                )
            return carry

        lax.fori_loop(0, members, update, 0)

        def send_reply(i, carry):
            peer = lax.rem(me + i, members)
            pltpu.make_async_remote_copy(
                reply.at[c, peer], out.at[c, me], reply_send, reply_recv,
                device_id={"member": peer}, device_id_type=MESH,
            ).start()
            return carry

        lax.fori_loop(1, members, send_reply, 0)
        out[c, me] = reply[c, me]

    blocks = (slice(None), pl.ds(0, members - 1))
    arrived(out.at[blocks], reply_recv)
    arrived(sent.at[blocks], fore_send)
    arrived(reply.at[blocks], reply_send)
    arrived(sums_in.at[pl.ds(0, members - 1)], sums_send)

    @pl.when(jnp.logical_not(first))
    def _():
        to_upper.wait_send()

    @pl.when(jnp.logical_not(last))
    def _():
        to_lower.wait_send()


def shards(
    starting_tracer_fields, surface_exchange_inputs, diffusivity, mixing, land_mask,
    obs_index, obs_count, obs_value, obs_error,
):
    members = lax.axis_size("member")
    domains = lax.axis_size("domain")
    _, fields, levels, rows, width = starting_tracer_fields.shape
    parts = fields * levels
    tile_rows = rows // members
    chunks = parts * tile_rows // SUB
    sums_width = pl.cdiv(2 * members + 1, LANES) * LANES
    halo_rows = pl.cdiv(2 * (parts + fields), SUB) * SUB
    tiles, slots = obs_index.shape[1:]
    f32, i32 = jnp.float32, jnp.int32
    vmem = pltpu.VMEM
    dma = pltpu.SemaphoreType.DMA
    window = 2 * SUB
    blocks = (chunks, members, SUB, width)
    anywhere = pl.BlockSpec(memory_space=pl.ANY)
    scalars = pl.BlockSpec(memory_space=pltpu.SMEM)
    result = pl.pallas_call(
        functools.partial(body, members, domains),
        out_shape=jax.ShapeDtypeStruct(blocks, f32),
        in_specs=[anywhere] * 6 + [scalars] * 3,
        out_specs=pl.BlockSpec(memory_space=pltpu.VMEM),
        scratch_shapes=[
            vmem((parts, rows, width), f32),
            vmem((fields, rows, width), f32),
            vmem((rows + 2 * SUB, width), i32),
            vmem((tiles, slots), i32),
            vmem((tiles, slots), f32),
            vmem((tiles, slots), f32),
            vmem((parts, rows, width), f32),
            vmem((parts, rows, width), f32),
            vmem((5, rows, width), f32),
            vmem((2, halo_rows, width), f32),
            vmem((2, halo_rows, width), f32),
            vmem((parts, window, width), f32),
            vmem((parts, window, width), f32),
            vmem((fields, window, width), f32),
            vmem((5, window, width), f32),
            vmem(blocks, f32),
            vmem(blocks, f32),
            vmem((sums_width, width), f32),
            vmem((members, sums_width), f32),
            vmem((members, members, sums_width), f32),
            vmem((members, members, LANES), f32),
            vmem((SUB, width), f32),
            vmem(blocks, f32),
            dma((8,)),
            dma((2,)),
            dma((2,)),
            dma,
            dma((chunks,)),
            dma,
            dma,
            dma,
            dma,
        ],
        compiler_params=pltpu.CompilerParams(
            collective_id=0, has_side_effects=True, vmem_limit_bytes=56 * 1024 * 1024
        ),
    )(
        starting_tracer_fields.reshape(parts, rows, width),
        surface_exchange_inputs.reshape(fields, rows, width),
        land_mask,
        obs_index.reshape(tiles, slots),
        obs_value.reshape(tiles, slots),
        obs_error.reshape(tiles, slots),
        obs_count.reshape(1, tiles),
        diffusivity,
        mixing,
    )
    result = result.reshape(chunks, members, SUB // tile_rows, tile_rows, width)
    result = jnp.swapaxes(result, 1, 2)
    return result.reshape(starting_tracer_fields.shape)


def solution(mesh):
    placed = (
        P("member", None, None, "domain", None),
        P("member", None, "domain", None),
        P(),
        P(),
        P(),
        P("domain", None, None),
        P("domain", None),
        P("domain", None, None),
        P("domain", None, None),
    )
    return jax.shard_map(
        shards,
        mesh=mesh,
        in_specs=placed,
        out_specs=P("member", None, None, "domain", None),
        check_vma=False,
    )
```

time: 90.7 us -> 42.2 us (0.47)
  Pallas kernels: 0 us -> 39.1 us
  blocking collectives: 37.3 us -> 0 us
  waiting for transfers between devices: 16.7 us -> 0 us
  starting transfers between devices: 16.6 us -> 0 us
  local copies, waits for them, and re-layouts: 10.7 us -> 2.85 us
  other arithmetic: 6.05 us -> 0 us
  matrix products: 2.55 us -> 0 us
    pallas_call x0 -> x1, Pallas kernels: none -> 39.1 us  [shards(): pl.pallas_call(functools.partial(body, members, domains), out_shape=jax.S...]
    psum x1 -> x0, blocking collectives: 20.4 us -> none  [shards(): gram, pull = lax.psum((gram, pull), 'member')]
    all_to_all x1 -> x0, blocking collectives: 16.9 us -> none  [shards(): lax.all_to_all(updated, 'member', split_axis=0, concat_axis=2, tiled=True)]
    all_to_all x1 -> x0, waiting for transfers between devices: 15.9 us -> none  [shards(): lax.all_to_all(stacked, 'member', split_axis=2, concat_axis=0, tiled=True)]
    ppermute x4 -> x0, starting transfers between devices: 10.8 us -> none  [the longest x2 8.18 us: with_halo(): before = lax.ppermute(last, axis, up)]
    all_to_all x1 -> x0, starting transfers between devices: 5.81 us -> none  [shards(): lax.all_to_all(stacked, 'member', split_axis=2, concat_axis=0, tiled=True)]
    slice x10 -> x0, local copies, waits for them, and re-layouts: 3.11 us -> none  [the longest x4 1.64 us: stencil(): west_cell = jnp.roll(middle, 1, axis=3)]
    another operation x5 -> x0, other arithmetic: 2.76 us -> none  [the longest x3 1.49 us: transform(): factor = jnp.linalg.cholesky(gram + (count - 1.0) * identity)]
  transfers between devices with their start and end apart: 5 -> 0, of which waited for: 2 -> 0; matrix products, arithmetic and copies ran while one was open for 4% -> 0% of each run, Pallas kernels for 0% -> 0%
where the time goes in v1:
time: 42.2 us; the launch traced here: 42 us
  Pallas kernels  39.1 us (93%)
  local copies, waits for them, and re-layouts  2.85 us (7%)
    pallas_call x1, Pallas kernels, shards(): pl.pallas_call(functools.partial(body, members, domains), out_shape=jax.S...  39.1 us
    reshape x1, local copies, waits for them, and re-layouts, shards(): result = result.reshape(chunks, members, SUB // tile_rows, tile_rows, width)  1.47 us
    reshape x1, local copies, waits for them, and re-layouts, shards(): return result.reshape(starting_tracer_fields.shape)  1.29 us

profile of v1, /device:TPU:0, one launch (start us, length us, event | category | flops | bytes accessed | tf_op | source)
XLA Modules:
  0.0 42.0 jit_solution(278383826532727800)
XLA Ops:
  0.0 39.1 %shard_map.91 = f32[4,8,8,640]{3,2,1,0:T(8,128)} custom-call(f32[16,16,640]{2,1,0:T(8,128)} %bitcast.9, f32[2,16,640]{2,1,0:T(8,128)} %bitcast.10, s32[64,640]{1,0:T(8,128)} %mask_hbm.1, s32[8,256]{1,0:T(8,128)} %bitcast.11, f32[8,256]{1,0:T(8,128)} %bitcast.12, f32[8,256]{1,0:T(8,128)} %bitcast.13, s32[1,8]{1,0:T(1,128)} %count.1, f32[2,8]{1,0:T(2,128)} %diffusivity.1, ...), custom_call_target="tpu_custom_call" | custom-call | tf_op jit(solution)/shard_map/pallas_call | solution.py:371
  39.1 1.5 %reshape.26 = f32[4,8,4,2,640]{4,3,2,1,0:T(2,128)S(1)} reshape(f32[4,8,8,640]{3,2,1,0:T(8,128)} %shard_map.91) | data formatting | bytes 1310720 | tf_op jit(solution)/shard_map/reshape | solution.py:424
  40.6 0.1 copy.10
  40.7 1.3 %reshape.27 = f32[1,2,8,16,640]{4,3,2,1,0:T(8,128)} reshape(f32[4,4,8,2,640]{4,3,2,1,0:T(2,128)S(1)} %copy.10) | data formatting | bytes 1310720 | tf_op jit(solution)/shard_map/reshape | solution.py:426

commit v2 on v1

--- a/solution.py
+++ b/solution.py
@@ -56,7 +56,7 @@
     count, diffusivity, mixing, out,
     x, flux, land, index, value, error, mid, fore, table,
     halo_out, halo_in, edge, edge_mid, edge_flux, edge_table,
-    sent, got, rhs, sums_out, sums_in, spread, tile_mask, reply,
+    sent, got, rhs, sums_out, sums_in, spread, tile_mask, reply, back,
     load_sem, halo_send, halo_recv, fore_send, fore_recv,
     sums_send, sums_recv, reply_send, reply_recv,
 ):
@@ -325,16 +325,23 @@
         def send_reply(i, carry):
             peer = lax.rem(me + i, members)
             pltpu.make_async_remote_copy(
-                reply.at[c, peer], out.at[c, me], reply_send, reply_recv,
+                reply.at[c, peer], back.at[c, me], reply_send, reply_recv.at[c],
                 device_id={"member": peer}, device_id_type=MESH,
             ).start()
             return carry
 
         lax.fori_loop(1, members, send_reply, 0)
-        out[c, me] = reply[c, me]
+        back[c, me] = reply[c, me]
+
+    for c in range(chunks):
+        arrived(back.at[c, pl.ds(0, members - 1)], reply_recv.at[c])
+        for k in range(per_chunk):
+            for tile in range(members):
+                out[c * per_chunk + k, tile * tile_rows : (tile + 1) * tile_rows] = back[
+                    c, tile, k * tile_rows : (k + 1) * tile_rows
+                ]
 
     blocks = (slice(None), pl.ds(0, members - 1))
-    arrived(out.at[blocks], reply_recv)
     arrived(sent.at[blocks], fore_send)
     arrived(reply.at[blocks], reply_send)
     arrived(sums_in.at[pl.ds(0, members - 1)], sums_send)
@@ -370,7 +377,7 @@
     scalars = pl.BlockSpec(memory_space=pltpu.SMEM)
     result = pl.pallas_call(
         functools.partial(body, members, domains),
-        out_shape=jax.ShapeDtypeStruct(blocks, f32),
+        out_shape=pltpu.VMEM((parts, rows, width), f32),
         in_specs=[anywhere] * 6 + [scalars] * 3,
         out_specs=pl.BlockSpec(memory_space=pltpu.VMEM),
         scratch_shapes=[
@@ -397,6 +404,7 @@
             vmem((members, members, LANES), f32),
             vmem((SUB, width), f32),
             vmem(blocks, f32),
+            vmem(blocks, f32),
             dma((8,)),
             dma((2,)),
             dma((2,)),
@@ -405,7 +413,7 @@
             dma,
             dma,
             dma,
-            dma,
+            dma((chunks,)),
         ],
         compiler_params=pltpu.CompilerParams(
             collective_id=0, has_side_effects=True, vmem_limit_bytes=56 * 1024 * 1024
@@ -421,8 +429,6 @@
         diffusivity,
         mixing,
     )
-    result = result.reshape(chunks, members, SUB // tile_rows, tile_rows, width)
-    result = jnp.swapaxes(result, 1, 2)
     return result.reshape(starting_tracer_fields.shape)
 
 

time: 42.2 us -> 39.4 us (0.934)
  local copies, waits for them, and re-layouts: 2.85 us -> 0.84 us
  Pallas kernels: 39.1 us -> 38.4 us
    reshape x2 -> x0, local copies, waits for them, and re-layouts: 2.76 us -> none  [the longest x1 1.47 us: shards(): result = result.reshape(chunks, members, SUB // tile_rows, tile_rows, width)]
    unnamed x0 -> x1, local copies, waits for them, and re-layouts: none -> 0.84 us
    pallas_call x1, Pallas kernels: 39.1 us -> 38.4 us  [shards(): pl.pallas_call(functools.partial(body, members, domains), out_shape=pltpu...]
where the time goes in v2:
time: 39.4 us; the launch traced here: 39.2 us
  Pallas kernels  38.4 us (97%)
  local copies, waits for them, and re-layouts  0.84 us (2%)
    pallas_call x1, Pallas kernels, shards(): pl.pallas_call(functools.partial(body, members, domains), out_shape=pltpu...  38.4 us
    unnamed x1, local copies, waits for them, and re-layouts  0.84 us

profile of v2, /device:TPU:0, one launch (start us, length us, event | category | flops | bytes accessed | tf_op | source)
XLA Modules:
  0.0 39.2 jit_solution(1941371456767003583)
XLA Ops:
  0.0 38.4 %shard_map.91 = f32[16,16,640]{2,1,0:T(8,128)S(1)} custom-call(f32[16,16,640]{2,1,0:T(8,128)} %bitcast.7, f32[2,16,640]{2,1,0:T(8,128)} %bitcast.8, s32[64,640]{1,0:T(8,128)} %mask_hbm.1, s32[8,256]{1,0:T(8,128)} %bitcast.9, f32[8,256]{1,0:T(8,128)} %bitcast.10, f32[8,256]{1,0:T(8,128)} %bitcast.11, s32[1,8]{1,0:T(1,128)} %count.1, f32[2,8]{1,0:T(2,128)} %diffusivity.1, ...), custom_call_target="tpu_custom_call" | custom-call | tf_op jit(solution)/shard_map/pallas_call | solution.py:378
  38.4 0.8 %copy.11 = f32[1,2,8,16,640]{4,3,2,1,0:T(8,128)} copy(f32[1,2,8,16,640]{4,3,2,1,0:T(8,128)S(1)} %bitcast.6) | data formatting | bytes 1310720

commit v3 on v2

--- a/solution.py
+++ b/solution.py
@@ -24,31 +24,26 @@
     table[4] = pltpu.roll(mask, 1, 1)
 
 
-def step(source, target, table, flux, diffusivity, mixing):
-    fields, levels = diffusivity.shape
+def step(f, source, target, table, flux, diffusivity, mixing):
+    levels = diffusivity.shape[1]
     rows, width = source.shape[1:]
-
-    def one(f, carry):
-        above = None
-        for l in range(levels):
-            x = source[f * levels + l]
-            lateral = table[1] * (pltpu.roll(x, rows - 1, 0) - x)
-            lateral += table[2] * (pltpu.roll(x, 1, 0) - x)
-            lateral += table[3] * (pltpu.roll(x, width - 1, 1) - x)
-            lateral += table[4] * (pltpu.roll(x, 1, 1) - x)
-            change = diffusivity[f, l] * lateral
-            if l < levels - 1:
-                down = mixing[f, l] * (source[f * levels + l + 1] - x)
-                change += down
-            if l > 0:
-                change -= above
-            else:
-                change += flux[f]
-            above = down
-            target[f * levels + l] = x + table[0] * change
-        return carry
-
-    lax.fori_loop(0, fields, one, 0)
+    above = None
+    for l in range(levels):
+        x = source[f * levels + l]
+        lateral = table[1] * (pltpu.roll(x, rows - 1, 0) - x)
+        lateral += table[2] * (pltpu.roll(x, 1, 0) - x)
+        lateral += table[3] * (pltpu.roll(x, width - 1, 1) - x)
+        lateral += table[4] * (pltpu.roll(x, 1, 1) - x)
+        change = diffusivity[f, l] * lateral
+        if l < levels - 1:
+            down = mixing[f, l] * (source[f * levels + l + 1] - x)
+            change += down
+        if l > 0:
+            change -= above
+        else:
+            change += flux[f]
+        above = down
+        target[f * levels + l] = x + table[0] * change
 
 
 def body(
@@ -63,7 +58,7 @@
     me = lax.axis_index("member")
     domain = lax.axis_index("domain")
     parts, rows, width = x.shape
-    fields = flux.shape[0]
+    fields, levels = diffusivity.shape
     chunks = got.shape[0]
     tile_rows = rows // members
     per_chunk = SUB // tile_rows
@@ -73,6 +68,23 @@
     start_row = pl.multiple_of(domain * rows, SUB)
     above_row = pl.multiple_of(jnp.maximum(domain * rows - SUB, 0), SUB)
     below_row = pl.multiple_of(jnp.minimum(domain * rows + rows, lat - SUB), SUB)
+
+    barrier = pltpu.get_barrier_semaphore()
+
+    def greet(i, carry):
+        peer = lax.rem(me + i, members)
+        pl.semaphore_signal(barrier, inc=1, device_id={"member": peer}, device_id_type=MESH)
+        return carry
+
+    @pl.when(jnp.logical_not(first))
+    def _():
+        pl.semaphore_signal(barrier, inc=1, device_id={"domain": domain - 1}, device_id_type=MESH)
+
+    @pl.when(jnp.logical_not(last))
+    def _():
+        pl.semaphore_signal(barrier, inc=1, device_id={"domain": domain + 1}, device_id_type=MESH)
+
+    lax.fori_loop(1, members, greet, 0)
 
     loads = [
         pltpu.make_async_copy(a, b, load_sem.at[i])
@@ -90,65 +102,57 @@
     for load in loads:
         load.start()
 
-    barrier = pltpu.get_barrier_semaphore()
-
-    def greet(i, carry):
-        peer = lax.rem(me + i, members)
-        pl.semaphore_signal(barrier, inc=1, device_id={"member": peer}, device_id_type=MESH)
-        return carry
-
-    @pl.when(jnp.logical_not(first))
-    def _():
-        pl.semaphore_signal(barrier, inc=1, device_id={"domain": domain - 1}, device_id_type=MESH)
-
-    @pl.when(jnp.logical_not(last))
-    def _():
-        pl.semaphore_signal(barrier, inc=1, device_id={"domain": domain + 1}, device_id_type=MESH)
-
-    lax.fori_loop(1, members, greet, 0)
     for load in loads:
         load.wait()
 
-    for p in range(parts):
-        halo_out[0, 2 * p : 2 * p + 2] = x[p, 0:2]
-        halo_out[1, 2 * p : 2 * p + 2] = x[p, rows - 2 : rows]
     for f in range(fields):
-        at = 2 * (parts + f)
-        halo_out[0, at : at + 2] = flux[f, 0:2]
-        halo_out[1, at : at + 2] = flux[f, rows - 2 : rows]
+        for l in range(levels + 1):
+            line = x.at[f * levels + l] if l < levels else flux.at[f]
+            halo_out[0, f, 2 * l : 2 * l + 2] = line[0:2]
+            halo_out[1, f, 2 * l : 2 * l + 2] = line[rows - 2 : rows]
     masks(land[SUB : SUB + rows].astype(jnp.float32), table)
-    step(x, mid, table, flux, diffusivity, mixing)
-    step(mid, fore, table, flux, diffusivity, mixing)
-
-    def pack(tile):
-        for p in range(parts):
+
+    def pack(tile, f):
+        for p in range(f * levels, (f + 1) * levels):
             k = (p % per_chunk) * tile_rows
             sent[p // per_chunk, tile, k : k + tile_rows] = fore[
                 p, tile * tile_rows : (tile + 1) * tile_rows
             ]
 
-    for tile in range(1, members - 1):
-        pack(tile)
-
+    def interior(f):
+        step(f, x, mid, table, flux, diffusivity, mixing)
+        step(f, mid, fore, table, flux, diffusivity, mixing)
+        for tile in range(1, members - 1):
+            pack(tile, f)
+
+    interior(0)
     greeted = members - 1 + (1 - first.astype(jnp.int32)) + (1 - last.astype(jnp.int32))
     pl.semaphore_wait(barrier, greeted)
 
-    to_upper = pltpu.make_async_remote_copy(
-        halo_out.at[0], halo_in.at[1], halo_send.at[0], halo_recv.at[1],
-        device_id={"domain": jnp.maximum(domain - 1, 0)}, device_id_type=MESH,
-    )
-    to_lower = pltpu.make_async_remote_copy(
-        halo_out.at[1], halo_in.at[0], halo_send.at[1], halo_recv.at[0],
-        device_id={"domain": jnp.minimum(domain + 1, domains - 1)}, device_id_type=MESH,
-    )
+    to_upper = [
+        pltpu.make_async_remote_copy(
+            halo_out.at[0, f], halo_in.at[1, f], halo_send.at[0, f], halo_recv.at[1, f],
+            device_id={"domain": jnp.maximum(domain - 1, 0)}, device_id_type=MESH,
+        )
+        for f in range(fields)
+    ]
+    to_lower = [
+        pltpu.make_async_remote_copy(
+            halo_out.at[1, f], halo_in.at[0, f], halo_send.at[1, f], halo_recv.at[0, f],
+            device_id={"domain": jnp.minimum(domain + 1, domains - 1)}, device_id_type=MESH,
+        )
+        for f in range(fields)
+    ]
 
     @pl.when(jnp.logical_not(first))
     def _():
-        to_upper.start()
+        for copy in to_upper:
+            copy.start()
 
     @pl.when(jnp.logical_not(last))
     def _():
-        to_lower.start()
+        for copy in to_lower:
+            copy.start()
 
     def send(chunk, peer):
         pltpu.make_async_remote_copy(
@@ -156,11 +160,11 @@
             device_id={"member": peer}, device_id_type=MESH,
         ).start()
 
-    early = (chunks + 1) // 2
+    early = chunks // fields
 
     def send_all(low, high, wanted):
         def one(i, carry):
-            chunk = low + i // (members - 1)
+            chunk = i // (members - 1)
             peer = lax.rem(me + 1 + lax.rem(i, members - 1), members)
 
             @pl.when(wanted(peer))
@@ -169,9 +173,13 @@
 
             return carry
 
-        lax.fori_loop(0, (high - low) * (members - 1), one, 0)
-
-    send_all(0, early, lambda t: jnp.logical_and(t > 0, t < members - 1))
+        lax.fori_loop(low, high, one, 0)
+
+    turn = members - 1
+    ahead = turn
+    inner = lambda t: jnp.logical_and(t > 0, t < members - 1)
+    outer = lambda t: jnp.logical_or(t == 0, t == members - 1)
+    send_all(0, ahead, inner)
 
     @pl.when(first)
     def _():
@@ -198,29 +206,33 @@
         edge_flux[f, 2:half] = flux[f, 0:6]
         edge_flux[f, half : half + 6] = flux[f, rows - 6 : rows]
 
-    @pl.when(jnp.logical_not(first))
-    def _():
-        to_lower.wait_recv()
-
-    @pl.when(jnp.logical_not(last))
-    def _():
-        to_upper.wait_recv()
-
-    for p in range(parts):
-        edge[p, 0:2] = halo_in[0, 2 * p : 2 * p + 2]
-        edge[p, half + 6 : half + 8] = halo_in[1, 2 * p : 2 * p + 2]
+    for f in range(1, fields):
+        interior(f)
+
     for f in range(fields):
-        at = 2 * (parts + f)
-        edge_flux[f, 0:2] = halo_in[0, at : at + 2]
-        edge_flux[f, half + 6 : half + 8] = halo_in[1, at : at + 2]
-    step(edge, edge_mid, edge_table, edge_flux, diffusivity, mixing)
-    step(edge_mid, edge, edge_table, edge_flux, diffusivity, mixing)
-    for p in range(parts):
-        fore[p, 0:2] = edge[p, 2:4]
-        fore[p, rows - 2 : rows] = edge[p, half + 4 : half + 6]
-    pack(0)
-    pack(members - 1)
-    send_all(0, early, lambda t: jnp.logical_or(t == 0, t == members - 1))
+
+        @pl.when(jnp.logical_not(first))
+        def _():
+            to_lower[f].wait_recv()
+
+        @pl.when(jnp.logical_not(last))
+        def _():
+            to_upper[f].wait_recv()
+
+        for l in range(levels + 1):
+            line = edge.at[f * levels + l] if l < levels else edge_flux.at[f]
+            line[0:2] = halo_in[0, f, 2 * l : 2 * l + 2]
+            line[half + 6 : half + 8] = halo_in[1, f, 2 * l : 2 * l + 2]
+        step(f, edge, edge_mid, edge_table, edge_flux, diffusivity, mixing)
+        step(f, edge_mid, edge, edge_table, edge_flux, diffusivity, mixing)
+        for p in range(f * levels, (f + 1) * levels):
+            fore[p, 0:2] = edge[p, 2:4]
+            fore[p, rows - 2 : rows] = edge[p, half + 4 : half + 6]
+        pack(0, f)
+        pack(members - 1, f)
+        if f == 0:
+            send_all(0, ahead, outer)
+            send_all(ahead, early * turn, lambda t: t >= 0)
     for c in range(chunks):
         got[c, me] = sent[c, me]
 
@@ -273,7 +285,7 @@
         return carry
 
     lax.fori_loop(1, members, send_sums, 0)
-    send_all(early, chunks, lambda t: t >= 0)
+    send_all(early * turn, chunks * turn, lambda t: t >= 0)
     arrived(sums_in.at[pl.ds(0, members - 1)], sums_recv)
 
     total = sums_in[0]
@@ -348,11 +360,13 @@
 
     @pl.when(jnp.logical_not(first))
     def _():
-        to_upper.wait_send()
+        for copy in to_upper:
+            copy.wait_send()
 
     @pl.when(jnp.logical_not(last))
     def _():
-        to_lower.wait_send()
+        for copy in to_lower:
+            copy.wait_send()
 
 
 def shards(
@@ -366,7 +380,7 @@
     tile_rows = rows // members
     chunks = parts * tile_rows // SUB
     sums_width = pl.cdiv(2 * members + 1, LANES) * LANES
-    halo_rows = pl.cdiv(2 * (parts + fields), SUB) * SUB
+    halo_rows = pl.cdiv(2 * (levels + 1), SUB) * SUB
     tiles, slots = obs_index.shape[1:]
     f32, i32 = jnp.float32, jnp.int32
     vmem = pltpu.VMEM
@@ -390,8 +404,8 @@
             vmem((parts, rows, width), f32),
             vmem((parts, rows, width), f32),
             vmem((5, rows, width), f32),
-            vmem((2, halo_rows, width), f32),
-            vmem((2, halo_rows, width), f32),
+            vmem((2, fields, halo_rows, width), f32),
+            vmem((2, fields, halo_rows, width), f32),
             vmem((parts, window, width), f32),
             vmem((parts, window, width), f32),
             vmem((fields, window, width), f32),
@@ -406,8 +420,8 @@
             vmem(blocks, f32),
             vmem(blocks, f32),
             dma((8,)),
-            dma((2,)),
-            dma((2,)),
+            dma((2, fields)),
+            dma((2, fields)),
             dma,
             dma((chunks,)),
             dma,

time: 39.4 us -> 37.7 us (0.957)
  the two profiles are of different devices: /device:TPU:0 before, /device:TPU:1 now
where the time goes in v3:
time: 37.7 us; the launch traced here: 37.5 us
  Pallas kernels  36.7 us (97%)
  local copies, waits for them, and re-layouts  0.84 us (2%)
    pallas_call x1, Pallas kernels, shards(): pl.pallas_call(functools.partial(body, members, domains), out_shape=pltpu...  36.7 us
    unnamed x1, local copies, waits for them, and re-layouts  0.84 us

profile of v3, /device:TPU:1, one launch (start us, length us, event | category | flops | bytes accessed | tf_op | source)
XLA Modules:
  0.0 37.5 jit_solution(14509288250015205060)
XLA Ops:
  0.0 36.7 %shard_map.91 = f32[16,16,640]{2,1,0:T(8,128)S(1)} custom-call(f32[16,16,640]{2,1,0:T(8,128)} %bitcast.7, f32[2,16,640]{2,1,0:T(8,128)} %bitcast.8, s32[64,640]{1,0:T(8,128)} %mask_hbm.1, s32[8,256]{1,0:T(8,128)} %bitcast.9, f32[8,256]{1,0:T(8,128)} %bitcast.10, f32[8,256]{1,0:T(8,128)} %bitcast.11, s32[1,8]{1,0:T(1,128)} %count.1, f32[2,8]{1,0:T(2,128)} %diffusivity.1, ...), custom_call_target="tpu_custom_call" | custom-call | tf_op jit(solution)/shard_map/pallas_call | solution.py:392
  36.7 0.8 %copy.11 = f32[1,2,8,16,640]{4,3,2,1,0:T(8,128)} copy(f32[1,2,8,16,640]{4,3,2,1,0:T(8,128)S(1)} %bitcast.6) | data formatting | bytes 1310720
